TPU v7x, 128 devices: a whole 4x4x4 slice. The times are simulated.
128 devices in a mesh: row: 8 (over z, core), col: 16 (over y, x).
Axes of the slice: x: 4, y: 4, z: 4, core: 2. Of those that a mesh axis runs over, the one named last changes fastest.
Arguments:
- front_diag: float32 [1024, 1024], replicated, may hold values from -4 to 16, as said below
- panel_rows: float32 [16384, 1024], P(('row', 'col')), may hold values from -1.2 to 1.2
- trailing: float32 [16384, 16384], P('row', 'col'), may hold values from -6 to 6
- pattern: int32 [64, 64], P('row', 'col'), may hold values 0 or 1
Outputs:
- diag_factor: float32 [1024, 1024], replicated
- panel_factor: float32 [16384, 1024], P(('row', 'col'))
- schur: float32 [16384, 16384], P('row', 'col')
Inputs may be any that keep to these rules, and one draw needn't show every extreme that they name: front_diag is symmetric and positive definite, with smallest eigenvalue at least 0.5.
All inputs are finite; a program needn't handle non-finite values. No bound on the sum of `pattern` on one device may be relied on, other than what follows from the above.
Results may differ from a plain program's by a relative error of at most 0.0003.
Values sent between devices are 32-bit elements; how exact they have to be, the bound alone decides.
A program may use at most 128 MiB of HBM per device.

v0:
```python
import jax
import jax.numpy as jnp
from jax import lax
from jax.sharding import PartitionSpec as P

BLOCK = 256


def spread(block, axis, holder):
    block = jnp.where(lax.axis_index(axis) == holder, block, jnp.zeros_like(block))
    return lax.psum(block, axis)


def column_rows(row_part, col_rows):
    ratio = lax.axis_size("col") // lax.axis_size("row")
    offset = lax.axis_index("col") % ratio * col_rows
    return lax.dynamic_slice_in_dim(row_part, offset, col_rows, 0)


def local(front_diag, panel_rows, trailing, pattern):
    diag_factor = jnp.linalg.cholesky(front_diag)
    panel_factor = jax.scipy.linalg.solve_triangular(diag_factor, panel_rows.T, lower=True).T
    local_rows = trailing.shape[0]
    col_rows = trailing.shape[1]
    ratio = lax.axis_size("col") // lax.axis_size("row")
    root_row = lax.axis_index("col") // ratio
    row_part = lax.all_gather(panel_factor, "col", axis=0, tiled=True)
    piece = column_rows(row_part, col_rows)
    col_part = spread(piece, "row", root_row)
    update = jnp.dot(row_part, col_part.T, precision=lax.Precision.HIGHEST)
    row_blocks = local_rows // BLOCK
    col_blocks = col_rows // BLOCK
    row_index = lax.axis_index("row") * row_blocks + jnp.arange(row_blocks)
    col_index = lax.axis_index("col") * col_blocks + jnp.arange(col_blocks)
    lower = (row_index[:, None] >= col_index[None, :]).astype(jnp.float32)
    keep = pattern.astype(jnp.float32) * lower
    masked = update.reshape(row_blocks, BLOCK, col_blocks, BLOCK) * keep[:, None, :, None]
    schur = trailing - masked.reshape(local_rows, col_rows)
    return (diag_factor, panel_factor, schur)


def solution(mesh):
    return jax.shard_map(
        local,
        mesh=mesh,
        in_specs=(P(), P(("row", "col"), None), P("row", "col"), P("row", "col")),
        out_specs=(P(), P(("row", "col"), None), P("row", "col")),
        check_vma=False,
    )
```

profile of v0, /device:TPU:0, one launch (start us, length us, event | category | flops | bytes accessed | tf_op | source)
XLA Modules:
  0.0 537.7 jit_solution(12177218288238149050)
XLA Ops:
  7.2 5.3 copy.7
  12.6 4.4 fusion
  19.0 11.7 %cholesky.223 = f32[128,128]{1,0:T(8,128)S(1)} custom-call(f32[128,128]{1,0:T(8,128)S(1)} %cholesky.580), custom_call_target="Cholesky" | custom-call | tf_op jit(solution)/shard_map/jit(cholesky)/cholesky | solution.py:21
  30.8 9.8 %custom-call.63 = f32[1,128,128]{1,2,0:T(8,128)S(1)} custom-call(f32[1,128,128]{2,1,0:T(8,128)S(1)} %get-tuple-element.61), custom_call_target="InvertDiagBlocksLowerTriangular" | custom-call | tf_op jit(solution)/shard_map/jit(cholesky)/cholesky | solution.py:21
  40.6 2.5 cholesky.255
  43.1 2.3 constant_dynamic-update-slice_fusion.32
  47.0 11.9 %cholesky.244 = f32[128,128]{1,0:T(8,128)S(1)} custom-call(f32[128,128]{1,0:T(8,128)S(1)} %cholesky.584), custom_call_target="Cholesky" | custom-call | tf_op jit(solution)/shard_map/jit(cholesky)/cholesky | solution.py:21
  59.5 9.8 %custom-call.64 = f32[1,128,128]{1,2,0:T(8,128)S(1)} custom-call(f32[1,128,128]{2,1,0:T(8,128)S(1)} %get-tuple-element.58), custom_call_target="InvertDiagBlocksLowerTriangular" | custom-call | tf_op jit(solution)/shard_map/jit(cholesky)/cholesky | solution.py:21
  72.7 11.7 %cholesky.468 = f32[128,128]{1,0:T(8,128)S(1)} custom-call(f32[128,128]{1,0:T(8,128)S(1)} %cholesky.589), custom_call_target="Cholesky" | custom-call | tf_op jit(solution)/shard_map/jit(cholesky)/cholesky | solution.py:21
  85.7 9.8 %custom-call.65 = f32[1,128,128]{1,2,0:T(8,128)S(1)} custom-call(f32[1,128,128]{2,1,0:T(8,128)S(1)} %get-tuple-element.55), custom_call_target="InvertDiagBlocksLowerTriangular" | custom-call | tf_op jit(solution)/shard_map/jit(cholesky)/cholesky | solution.py:21
  96.6 2.3 convolution_subtract_fusion.2
  99.0 11.9 %cholesky.487 = f32[128,128]{1,0:T(8,128)S(1)} custom-call(f32[128,128]{1,0:T(8,128)S(1)} %cholesky.594), custom_call_target="Cholesky" | custom-call | tf_op jit(solution)/shard_map/jit(cholesky)/cholesky | solution.py:21
  112.2 9.8 %custom-call.66 = f32[1,128,128]{1,2,0:T(8,128)S(1)} custom-call(f32[1,128,128]{2,1,0:T(8,128)S(1)} %get-tuple-element.52), custom_call_target="InvertDiagBlocksLowerTriangular" | custom-call | tf_op jit(solution)/shard_map/jit(cholesky)/cholesky | solution.py:21
  123.1 2.4 convolution_subtract_fusion.3
  125.4 11.7 %cholesky.506 = f32[128,128]{1,0:T(8,128)S(1)} custom-call(f32[128,128]{1,0:T(8,128)S(1)} %cholesky.599), custom_call_target="Cholesky" | custom-call | tf_op jit(solution)/shard_map/jit(cholesky)/cholesky | solution.py:21
  138.5 10.2 %custom-call.67 = f32[1,128,128]{1,2,0:T(8,128)S(1)} custom-call(f32[1,128,128]{2,1,0:T(8,128)S(1)} %get-tuple-element.49), custom_call_target="InvertDiagBlocksLowerTriangular" | custom-call | tf_op jit(solution)/shard_map/jit(cholesky)/cholesky | solution.py:21
  149.7 2.3 convolution_subtract_fusion.4
  152.0 11.7 %cholesky.526 = f32[128,128]{1,0:T(8,128)S(1)} custom-call(f32[128,128]{1,0:T(8,128)S(1)} %cholesky.604), custom_call_target="Cholesky" | custom-call | tf_op jit(solution)/shard_map/jit(cholesky)/cholesky | solution.py:21
  165.0 9.8 %custom-call.68 = f32[1,128,128]{1,2,0:T(8,128)S(1)} custom-call(f32[1,128,128]{2,1,0:T(8,128)S(1)} %get-tuple-element.46), custom_call_target="InvertDiagBlocksLowerTriangular" | custom-call | tf_op jit(solution)/shard_map/jit(cholesky)/cholesky | solution.py:21
  177.9 11.9 %cholesky.546 = f32[128,128]{1,0:T(8,128)S(1)} custom-call(f32[128,128]{1,0:T(8,128)S(1)} %cholesky.609), custom_call_target="Cholesky" | custom-call | tf_op jit(solution)/shard_map/jit(cholesky)/cholesky | solution.py:21
  191.0 9.8 %custom-call.69 = f32[1,128,128]{1,2,0:T(8,128)S(1)} custom-call(f32[1,128,128]{2,1,0:T(8,128)S(1)} %get-tuple-element.43), custom_call_target="InvertDiagBlocksLowerTriangular" | custom-call | tf_op jit(solution)/shard_map/jit(cholesky)/cholesky | solution.py:21
  203.4 11.7 %cholesky.564 = f32[128,128]{1,0:T(8,128)S(1)} custom-call(f32[128,128]{1,0:T(8,128)S(1)} %convolution_subtract_fusion.11), custom_call_target="Cholesky" | custom-call | tf_op jit(solution)/shard_map/jit(cholesky)/cholesky | solution.py:21
  222.0 6.8 %fusion.1 = (f32[1024,1024]{1,0:T(8,128)}, f32[1024,1024]{1,0:T(8,128)}) fusion(f32[1024,1024]{1,0:T(8,128)} %get-tuple-element.41, pred[]{:T(512)S(6)} %cholesky.579), kind=kLoop, calls=%fused_computation.8 | loop fusion | flops 4194304 | bytes 12582913 | tf_op jit(solution)/shard_map/jit(_solve_triangular)/triangular_solve | solution.py:22
  228.8 22.5 %while.1 = (s32[]{:T(128)}, f32[1024,1024]{1,0:T(8,128)}, s32[8,2]{0,1:T(2,128)S(1)}, f32[8,128,128]{2,1,0:T(8,128)S(1)}, s32[]{:T(128)}) while((s32[]{:T(128)}, f32[1024,1024]{1,0:T(8,128)}, s32[8,2]{0,1:T(2,128)S(1)}, f32[8,128,128]{2,1,0:T(8,128)S(1)}, s32[]{:T(128)}) %tuple.58), condition=%wide.while_cond, body=%wide.while_body.sunk | while | flops 2 | bytes 131189 | solution.py:22
  229.4 2.2 bitcast_dynamic-update-slice_fusion.2
  232.3 2.2 bitcast_dynamic-update-slice_fusion.2
  251.3 78.8 %custom-call.70 = f32[8,128,128]{1,2,0:T(8,128)S(1)} custom-call(f32[8,128,128]{2,1,0:T(8,128)S(1)} %get-tuple-element.10), custom_call_target="InvertDiagBlocksLowerTriangular" | custom-call | tf_op jit(solution)/shard_map/jit(_solve_triangular)/triangular_solve | solution.py:22
  344.9 73.2 %all-gather.2.cloned.1.call-done = f32[2048,1024]{1,0:T(8,128)} async-done(((f32[128,1024]{1,0:T(8,128)}), f32[2048,1024]{1,0:T(8,128)}) %all-gather.2.cloned.1.call-update) | async-done | bytes 8388624 | tf_op jit(solution)/shard_map/all_gather | solution.py:27
  418.1 5.0 dynamic-slice_select_fusion
  425.0 5.5 %copy.18 = f32[256,8,4,256]{3,1,2,0:T(8,128)} copy(f32[256,8,4,256]{3,2,1,0:T(4,128)S(1)} %bitcast.109) | data formatting | bytes 16777216
  430.5 65.2 %all-reduce.3.cloned.1.call-done = f32[1024,1024]{1,0:T(8,128)} async-done(((f32[1024,1024]{1,0:T(8,128)}), f32[1024,1024]{1,0:T(8,128)}) %all-reduce.3.cloned.1.call-update) | async-done | bytes 4194320 | tf_op jit(solution)/shard_map/psum | solution.py:11
  495.8 34.7 %multiply_subtract_fusion = f32[2048,1024]{1,0:T(8,128)} fusion(f32[2048,1024]{1,0:T(8,128)} %param.6, f32[2048,1024]{1,0:T(8,128)} %bitcast.108, f32[2048,1024]{1,0:T(8,128)} %all-gather.2.cloned.1.call-done, f32[1024,1024]{1,0:T(8,128)} %all-reduce.3.cloned.1.call-done), kind=kOutput, calls=%fused_computation.2 | convolution fusion | flops 25773998080 | bytes 37748736 | tf_op jit(solution)/shard_map/dot_general | solution.py:30
  (103 shorter events, 59.3 us)
Async XLA Ops:
  7.2 410.9 %all-gather.2.cloned.1.call-start = ((), (), s32[]{:S(2)}) async-start(), calls=%async_computation | async-start | bytes 8912896 | tf_op jit(solution)/shard_map/all_gather | solution.py:27
  17.0 2.0 copy-start
  222.0 108.2 %copy-start.2 = (f32[128,1024]{1,0:T(8,128)S(1)}, f32[128,1024]{1,0:T(8,128)}, u32[]{:S(2)}) copy-start(f32[128,1024]{1,0:T(8,128)} %param.5) | copy-start | bytes 1572868
  344.0 0.8 copy-start.1
  344.8 150.9 %all-reduce.3.cloned.1.call-start = ((), (), s32[]{:S(2)}) async-start(), calls=%async_computation.1 | async-start | bytes 8388608 | tf_op jit(solution)/shard_map/psum | solution.py:11
  423.1 0.7 copy-start.3
Sparse Core Ops, SparseCore 0:
  345.0 73.0 all-gather.1
  423.2 72.5 all-reduce.2
where the time goes:
time: 548 us; the launch traced here: 538 us
  other arithmetic  267 us (49%)
  waiting for transfers between devices  138 us (25%)
  matrix products  70.7 us (13%)
  local copies, waits for them, and re-layouts  41.1 us (8%)
  between operations  19.9 us (4%)
    another operation x30, other arithmetic, local(): diag_factor = jnp.linalg.cholesky(front_diag)  172 us
    another operation x3, other arithmetic, local(): jax.scipy.linalg.solve_triangular(diag_factor, panel_rows.T, lower=True)  85.7 us
    all_gather x1, waiting for transfers between devices, local(): row_part = lax.all_gather(panel_factor, 'col', axis=0, tiled=True)  73.2 us
    psum x1, waiting for transfers between devices, spread(): return lax.psum(block, axis)  65.2 us
    dot_general x1, matrix products, local(): update = jnp.dot(row_part, col_part.T, precision=lax.Precision.HIGHEST)  34.7 us
    another operation x14, matrix products, local(): diag_factor = jnp.linalg.cholesky(front_diag)  23 us
    another operation x24, local copies, waits for them, and re-layouts  22.4 us
    unnamed x17, local copies, waits for them, and re-layouts  14.3 us
  transfers between devices with their start and end apart: 2, of which 2 were waited for; matrix products, arithmetic and copies ran while one was open for 1% of the time, Pallas kernels for 0%

commit v1 on v0

--- a/solution.py
+++ b/solution.py
@@ -4,6 +4,12 @@
 from jax.sharding import PartitionSpec as P
 
 BLOCK = 256
+
+
+def in_order(parts, dim):
+    dims = list(parts.shape[1:])
+    dims[dim] *= parts.shape[0]
+    return jnp.moveaxis(parts, 0, dim).reshape(dims)
 
 
 def spread(block, axis, holder):
@@ -24,7 +30,19 @@
     col_rows = trailing.shape[1]
     ratio = lax.axis_size("col") // lax.axis_size("row")
     root_row = lax.axis_index("col") // ratio
-    row_part = lax.all_gather(panel_factor, "col", axis=0, tiled=True)
+    size = lax.axis_size("col")
+    pairs = [(i, (i + 1) % size) for i in range(size)]
+    back = [(b, a) for a, b in pairs]
+    lower_2, upper = ([], [])
+    for step in range(size - 1):
+        if step % 2 == 0:
+            lower_2.append(lax.ppermute(lower_2[-1] if lower_2 else panel_factor, "col", pairs))
+        else:
+            upper.append(lax.ppermute(upper[-1] if upper else panel_factor, "col", back))
+    tiles = jnp.stack([*lower_2[::-1], panel_factor, *upper])
+    shift = lax.axis_index("col") - len(lower_2)
+    tiles = tiles[(jnp.arange(size) - shift) % size]
+    row_part = in_order(tiles, 0)
     piece = column_rows(row_part, col_rows)
     col_part = spread(piece, "row", root_row)
     update = jnp.dot(row_part, col_part.T, precision=lax.Precision.HIGHEST)

time: 548 us -> 663 us (1.21)
  local copies, waits for them, and re-layouts: 41.1 us -> 111 us
  starting transfers between devices: 0.08 us -> 40.7 us
  other arithmetic: 267 us -> 279 us
    ppermute x0 -> x15, waiting for transfers between devices: none -> 73.2 us  [the longest x8 71.1 us: local(): lax.ppermute(lower_2[-1] if lower_2 else panel_factor, 'col', pairs)]
    all_gather x1 -> x0, waiting for transfers between devices: 73.2 us -> none  [local(): row_part = lax.all_gather(panel_factor, 'col', axis=0, tiled=True)]
    unnamed x17 -> x42, local copies, waits for them, and re-layouts: 14.3 us -> 57.9 us
    ppermute x0 -> x15, starting transfers between devices: none -> 40.6 us  [the longest x7 39 us: local(): lax.ppermute(upper[-1] if upper else panel_factor, 'col', back)]
    gather x0 -> x2, local copies, waits for them, and re-layouts: none -> 16.9 us  [local(): tiles = tiles[(jnp.arange(size) - shift) % size]]
    sub x0 -> x1, other arithmetic: none -> 11.7 us  [local(): schur = trailing - masked.reshape(local_rows, col_rows)]
    mul x1, local copies, waits for them, and re-layouts: 1.15 us -> 10.6 us  [local(): update.reshape(row_blocks, BLOCK, col_blocks, BLOCK)]
    another operation x24 -> x25, local copies, waits for them, and re-layouts: 22.4 us -> 23.2 us
  transfers between devices with their start and end apart: 2 -> 16, of which waited for: 2 -> 12; matrix products, arithmetic and copies ran while one was open for 1% -> 4% of each run, Pallas kernels for 0% -> 0%
where the time goes in v1:
time: 663 us; the launch traced here: 653 us
  other arithmetic  279 us (42%)
  waiting for transfers between devices  133 us (20%)
  local copies, waits for them, and re-layouts  111 us (17%)
  matrix products  68.6 us (10%)
  starting transfers between devices  40.7 us (6%)
  between operations  19.8 us (3%)
    another operation x30, other arithmetic, local(): diag_factor = jnp.linalg.cholesky(front_diag)  172 us
    another operation x3, other arithmetic, local(): jax.scipy.linalg.solve_triangular(diag_factor, panel_rows.T, lower=True)  85.6 us
    ppermute x8, waiting for transfers between devices, local(): lax.ppermute(lower_2[-1] if lower_2 else panel_factor, 'col', pairs)  71.1 us
    psum x1, waiting for transfers between devices, spread(): return lax.psum(block, axis)  59.5 us
    unnamed x42, local copies, waits for them, and re-layouts  57.9 us
    ppermute x7, starting transfers between devices, local(): lax.ppermute(upper[-1] if upper else panel_factor, 'col', back)  39 us
    dot_general x1, matrix products, local(): update = jnp.dot(row_part, col_part.T, precision=lax.Precision.HIGHEST)  32.5 us
    another operation x14, matrix products, local(): diag_factor = jnp.linalg.cholesky(front_diag)  23 us
  transfers between devices with their start and end apart: 16, of which 12 were waited for; matrix products, arithmetic and copies ran while one was open for 4% of the time, Pallas kernels for 0%

profile of v1, /device:TPU:0, one launch (start us, length us, event | category | flops | bytes accessed | tf_op | source)
XLA Modules:
  0.0 652.6 jit_solution(5319879922713346626)
XLA Ops:
  19.0 11.7 %cholesky.223 = f32[128,128]{1,0:T(8,128)S(1)} custom-call(f32[128,128]{1,0:T(8,128)S(1)} %cholesky.580), custom_call_target="Cholesky" | custom-call | tf_op jit(solution)/shard_map/jit(cholesky)/cholesky | solution.py:27
  30.8 9.8 %custom-call.63 = f32[1,128,128]{1,2,0:T(8,128)S(1)} custom-call(f32[1,128,128]{2,1,0:T(8,128)S(1)} %get-tuple-element.75), custom_call_target="InvertDiagBlocksLowerTriangular" | custom-call | tf_op jit(solution)/shard_map/jit(cholesky)/cholesky | solution.py:27
  47.0 12.0 %cholesky.244 = f32[128,128]{1,0:T(8,128)S(1)} custom-call(f32[128,128]{1,0:T(8,128)S(1)} %cholesky.584), custom_call_target="Cholesky" | custom-call | tf_op jit(solution)/shard_map/jit(cholesky)/cholesky | solution.py:27
  59.7 9.8 %custom-call.64 = f32[1,128,128]{1,2,0:T(8,128)S(1)} custom-call(f32[1,128,128]{2,1,0:T(8,128)S(1)} %get-tuple-element.72), custom_call_target="InvertDiagBlocksLowerTriangular" | custom-call | tf_op jit(solution)/shard_map/jit(cholesky)/cholesky | solution.py:27
  72.9 11.7 %cholesky.468 = f32[128,128]{1,0:T(8,128)S(1)} custom-call(f32[128,128]{1,0:T(8,128)S(1)} %cholesky.589), custom_call_target="Cholesky" | custom-call | tf_op jit(solution)/shard_map/jit(cholesky)/cholesky | solution.py:27
  85.8 9.8 %custom-call.65 = f32[1,128,128]{1,2,0:T(8,128)S(1)} custom-call(f32[1,128,128]{2,1,0:T(8,128)S(1)} %get-tuple-element.69), custom_call_target="InvertDiagBlocksLowerTriangular" | custom-call | tf_op jit(solution)/shard_map/jit(cholesky)/cholesky | solution.py:27
  99.2 11.8 %cholesky.487 = f32[128,128]{1,0:T(8,128)S(1)} custom-call(f32[128,128]{1,0:T(8,128)S(1)} %cholesky.594), custom_call_target="Cholesky" | custom-call | tf_op jit(solution)/shard_map/jit(cholesky)/cholesky | solution.py:27
  112.3 9.8 %custom-call.66 = f32[1,128,128]{1,2,0:T(8,128)S(1)} custom-call(f32[1,128,128]{2,1,0:T(8,128)S(1)} %get-tuple-element.66), custom_call_target="InvertDiagBlocksLowerTriangular" | custom-call | tf_op jit(solution)/shard_map/jit(cholesky)/cholesky | solution.py:27
  125.6 11.7 %cholesky.506 = f32[128,128]{1,0:T(8,128)S(1)} custom-call(f32[128,128]{1,0:T(8,128)S(1)} %cholesky.599), custom_call_target="Cholesky" | custom-call | tf_op jit(solution)/shard_map/jit(cholesky)/cholesky | solution.py:27
  138.6 10.0 %custom-call.67 = f32[1,128,128]{1,2,0:T(8,128)S(1)} custom-call(f32[1,128,128]{2,1,0:T(8,128)S(1)} %get-tuple-element.63), custom_call_target="InvertDiagBlocksLowerTriangular" | custom-call | tf_op jit(solution)/shard_map/jit(cholesky)/cholesky | solution.py:27
  152.0 11.7 %cholesky.526 = f32[128,128]{1,0:T(8,128)S(1)} custom-call(f32[128,128]{1,0:T(8,128)S(1)} %cholesky.604), custom_call_target="Cholesky" | custom-call | tf_op jit(solution)/shard_map/jit(cholesky)/cholesky | solution.py:27
  165.0 9.8 %custom-call.68 = f32[1,128,128]{1,2,0:T(8,128)S(1)} custom-call(f32[1,128,128]{2,1,0:T(8,128)S(1)} %get-tuple-element.60), custom_call_target="InvertDiagBlocksLowerTriangular" | custom-call | tf_op jit(solution)/shard_map/jit(cholesky)/cholesky | solution.py:27
  177.8 12.1 %cholesky.546 = f32[128,128]{1,0:T(8,128)S(1)} custom-call(f32[128,128]{1,0:T(8,128)S(1)} %cholesky.609), custom_call_target="Cholesky" | custom-call | tf_op jit(solution)/shard_map/jit(cholesky)/cholesky | solution.py:27
  191.2 9.8 %custom-call.69 = f32[1,128,128]{1,2,0:T(8,128)S(1)} custom-call(f32[1,128,128]{2,1,0:T(8,128)S(1)} %get-tuple-element.57), custom_call_target="InvertDiagBlocksLowerTriangular" | custom-call | tf_op jit(solution)/shard_map/jit(cholesky)/cholesky | solution.py:27
  203.6 11.7 %cholesky.564 = f32[128,128]{1,0:T(8,128)S(1)} custom-call(f32[128,128]{1,0:T(8,128)S(1)} %convolution_subtract_fusion.11), custom_call_target="Cholesky" | custom-call | tf_op jit(solution)/shard_map/jit(cholesky)/cholesky | solution.py:27
  222.2 6.8 %fusion.3 = (f32[1024,1024]{1,0:T(8,128)}, f32[1024,1024]{1,0:T(8,128)}) fusion(f32[1024,1024]{1,0:T(8,128)} %get-tuple-element.55, pred[]{:T(512)S(6)} %cholesky.579), kind=kLoop, calls=%fused_computation.11 | loop fusion | flops 4194304 | bytes 12582913 | tf_op jit(solution)/shard_map/jit(_solve_triangular)/triangular_solve | solution.py:28
  229.0 22.5 %while.1 = (s32[]{:T(128)}, f32[1024,1024]{1,0:T(8,128)}, s32[8,2]{0,1:T(2,128)S(1)}, f32[8,128,128]{2,1,0:T(8,128)S(1)}, s32[]{:T(128)}) while((s32[]{:T(128)}, f32[1024,1024]{1,0:T(8,128)}, s32[8,2]{0,1:T(2,128)S(1)}, f32[8,128,128]{2,1,0:T(8,128)S(1)}, s32[]{:T(128)}) %tuple.64), condition=%wide.while_cond, body=%wide.while_body.sunk | while | flops 2 | bytes 131181 | solution.py:28
  251.5 78.8 %custom-call.70 = f32[8,128,128]{1,2,0:T(8,128)S(1)} custom-call(f32[8,128,128]{2,1,0:T(8,128)S(1)} %get-tuple-element.10), custom_call_target="InvertDiagBlocksLowerTriangular" | custom-call | tf_op jit(solution)/shard_map/jit(_solve_triangular)/triangular_solve | solution.py:28
  345.2 15.6 %collective-permute-done = f32[128,1024]{0,1:T(8,128)S(1)} collective-permute-done((f32[128,1024]{0,1:T(8,128)S(1)}, f32[128,1024]{0,1:T(8,128)S(1)}, u32[]{:S(2)}, u32[]{:S(2)}) %collective-permute-start) | collective-permute-done | bytes 524320 | tf_op jit(solution)/shard_map/ppermute | solution.py:39
  366.1 11.0 %collective-permute-done.1 = f32[128,1024]{0,1:T(8,128)S(1)} collective-permute-done((f32[128,1024]{0,1:T(8,128)S(1)}, f32[128,1024]{0,1:T(8,128)S(1)}, u32[]{:S(2)}, u32[]{:S(2)}) %collective-permute-start.1) | collective-permute-done | bytes 524320 | tf_op jit(solution)/shard_map/ppermute | solution.py:39
  382.5 10.1 %collective-permute-done.2 = f32[128,1024]{0,1:T(8,128)S(1)} collective-permute-done((f32[128,1024]{0,1:T(8,128)S(1)}, f32[128,1024]{0,1:T(8,128)S(1)}, u32[]{:S(2)}, u32[]{:S(2)}) %collective-permute-start.2) | collective-permute-done | bytes 524320 | tf_op jit(solution)/shard_map/ppermute | solution.py:39
  398.0 9.2 %collective-permute-done.3 = f32[128,1024]{0,1:T(8,128)S(1)} collective-permute-done((f32[128,1024]{0,1:T(8,128)S(1)}, f32[128,1024]{0,1:T(8,128)S(1)}, u32[]{:S(2)}, u32[]{:S(2)}) %collective-permute-start.3) | collective-permute-done | bytes 524320 | tf_op jit(solution)/shard_map/ppermute | solution.py:39
  413.3 7.4 %collective-permute-done.4 = f32[128,1024]{0,1:T(8,128)S(1)} collective-permute-done((f32[128,1024]{0,1:T(8,128)S(1)}, f32[128,1024]{0,1:T(8,128)S(1)}, u32[]{:S(2)}, u32[]{:S(2)}) %collective-permute-start.4) | collective-permute-done | bytes 524320 | tf_op jit(solution)/shard_map/ppermute | solution.py:39
  478.7 7.7 %gather_fusion = f32[16,128,1024]{1,2,0:T(8,128)} fusion(f32[16,128,1024]{1,2,0:T(8,128)} %bitcast_dynamic-update-slice_fusion.2, s32[1024]{0:T(1024)S(1)} %pad_clamp_fusion), kind=kCustom, calls=%fused_computation | custom fusion | bytes 16777280 | tf_op jit(solution)/shard_map/gather | solution.py:44
  486.4 9.3 %copy.12 = f32[16,128,1024]{2,1,0:T(8,128)} copy(f32[16,128,1024]{1,2,0:T(8,128)} %gather_fusion) | data formatting | bytes 16777216 | tf_op jit(solution)/shard_map/gather | solution.py:44
  501.8 9.2 %copy.16 = f32[2048,1024]{0,1:T(8,128)} copy(f32[2048,1024]{1,0:T(8,128)} %param.6) | data formatting | bytes 16777216 | tf_op args[2]
  511.0 59.5 %all-reduce.3.cloned.1.call-done = f32[4,256,1024]{2,1,0:T(8,128)} async-done(((f32[4,256,1024]{2,1,0:T(8,128)}), f32[4,256,1024]{2,1,0:T(8,128)}) %all-reduce.3.cloned.1.call-update) | async-done | bytes 4194320 | tf_op jit(solution)/shard_map/psum | solution.py:17
  570.5 32.5 %broadcast_multiply_fusion = f32[8,256,4,256]{3,1,2,0:T(8,128)} fusion(f32[8,4]{1,0:T(8,128)S(1)} %copy.14, f32[8,256,1024,1]{2,1,3,0:T(8,128)} %bitcast.159, f32[4,256,1024]{2,1,0:T(8,128)} %all-reduce.3.cloned.1.call-done), kind=kOutput, calls=%fused_computation.7 | convolution fusion | flops 25771900928 | bytes 20971648 | tf_op jit(solution)/shard_map/dot_general | solution.py:48
  603.0 10.6 %copy.15 = f32[8,256,4,256]{1,0,3,2:T(8,128)} copy(f32[8,256,4,256]{3,1,2,0:T(8,128)} %broadcast_multiply_fusion) | data formatting | bytes 16777216 | tf_op jit(solution)/shard_map/mul | solution.py:55
  613.6 10.7 %copy.20 = f32[128,8,8,256]{3,1,2,0:T(8,128)} copy(f32[128,8,8,256]{3,2,1,0:T(8,128)} %bitcast.157) | data formatting | bytes 16777216
  624.3 11.7 %sub.27 = f32[2048,1024]{0,1:T(8,128)} subtract(f32[2048,1024]{0,1:T(8,128)} %copy.16, f32[2048,1024]{0,1:T(8,128)} %bitcast.156) | non-fusion elementwise | flops 2097152 | bytes 25165824 | tf_op jit(solution)/shard_map/sub | solution.py:56
  636.0 9.2 %copy.18 = f32[2048,1024]{1,0:T(8,128)} copy(f32[2048,1024]{0,1:T(8,128)} %sub.27) | data formatting | bytes 16777216
  (154 shorter events, 169.9 us)
Async XLA Ops:
  7.2 563.4 %all-reduce.3.cloned.1.call-start = ((), (), s32[]{:S(2)}) async-start(), calls=%async_computation | async-start | bytes 8388608 | tf_op jit(solution)/shard_map/psum | solution.py:17
  17.0 2.0 copy-start
  222.1 108.1 %copy-start.1 = (f32[128,1024]{1,0:T(8,128)S(1)}, f32[128,1024]{1,0:T(8,128)}, u32[]{:S(2)}) copy-start(f32[128,1024]{1,0:T(8,128)} %param.5) | copy-start | bytes 1572868
  343.5 17.3 %collective-permute-start = (f32[128,1024]{0,1:T(8,128)S(1)}, f32[128,1024]{0,1:T(8,128)S(1)}, u32[]{:S(2)}, u32[]{:S(2)}) collective-permute-start(f32[128,1024]{0,1:T(8,128)S(1)} %bitcast.161), channel_id=1, source_target_pairs={{0,1},{1,2},{2,3},{3,4},{4,5},{5,6},{6,7},{7,8},{8,9},{9,10},{10,1... | collective-permute-start | bytes 1572872 | tf_op jit(solution)/shard_map/ppermute | solution.py:39
  360.8 16.4 %collective-permute-start.1 = (f32[128,1024]{0,1:T(8,128)S(1)}, f32[128,1024]{0,1:T(8,128)S(1)}, u32[]{:S(2)}, u32[]{:S(2)}) collective-permute-start(f32[128,1024]{0,1:T(8,128)S(1)} %collective-permute-done), channel_id=1, source_target_pairs={{0,1},{1,2},{2,3},{3,4},{4,5},{5,6},{6,7},{7,8},{8,9},{9,10},{10,1... | collective-permute-start | bytes 1572872 | tf_op jit(solution)/shard_map/ppermute | solution.py:39
  360.8 16.4 %collective-permute-start.8 = (f32[128,1024]{0,1:T(8,128)S(1)}, f32[128,1024]{0,1:T(8,128)S(1)}, u32[]{:S(2)}, u32[]{:S(2)}) collective-permute-start(f32[128,1024]{0,1:T(8,128)S(1)} %bitcast.162), channel_id=1, source_target_pairs={{1,0},{2,1},{3,2},{4,3},{5,4},{6,5},{7,6},{8,7},{9,8},{10,9},{11,1... | collective-permute-start | bytes 1572872 | tf_op jit(solution)/shard_map/ppermute | solution.py:41
  377.2 15.5 %collective-permute-start.2 = (f32[128,1024]{0,1:T(8,128)S(1)}, f32[128,1024]{0,1:T(8,128)S(1)}, u32[]{:S(2)}, u32[]{:S(2)}) collective-permute-start(f32[128,1024]{0,1:T(8,128)S(1)} %collective-permute-done.1), channel_id=1, source_target_pairs={{0,1},{1,2},{2,3},{3,4},{4,5},{5,6},{6,7},{7,8},{8,9},{9,10},{10,1... | collective-permute-start | bytes 1572872 | tf_op jit(solution)/shard_map/ppermute | solution.py:39
  377.2 15.5 %collective-permute-start.9 = (f32[128,1024]{0,1:T(8,128)S(1)}, f32[128,1024]{0,1:T(8,128)S(1)}, u32[]{:S(2)}, u32[]{:S(2)}) collective-permute-start(f32[128,1024]{0,1:T(8,128)S(1)} %collective-permute-done.8), channel_id=1, source_target_pairs={{1,0},{2,1},{3,2},{4,3},{5,4},{6,5},{7,6},{8,7},{9,8},{10,9},{11,1... | collective-permute-start | bytes 1572872 | tf_op jit(solution)/shard_map/ppermute | solution.py:41
  392.6 14.5 %collective-permute-start.3 = (f32[128,1024]{0,1:T(8,128)S(1)}, f32[128,1024]{0,1:T(8,128)S(1)}, u32[]{:S(2)}, u32[]{:S(2)}) collective-permute-start(f32[128,1024]{0,1:T(8,128)S(1)} %collective-permute-done.2), channel_id=1, source_target_pairs={{0,1},{1,2},{2,3},{3,4},{4,5},{5,6},{6,7},{7,8},{8,9},{9,10},{10,1... | collective-permute-start | bytes 1572872 | tf_op jit(solution)/shard_map/ppermute | solution.py:39
  392.6 14.5 %collective-permute-start.10 = (f32[128,1024]{0,1:T(8,128)S(1)}, f32[128,1024]{0,1:T(8,128)S(1)}, u32[]{:S(2)}, u32[]{:S(2)}) collective-permute-start(f32[128,1024]{0,1:T(8,128)S(1)} %collective-permute-done.9), channel_id=1, source_target_pairs={{1,0},{2,1},{3,2},{4,3},{5,4},{6,5},{7,6},{8,7},{9,8},{10,9},{11,1... | collective-permute-start | bytes 1572872 | tf_op jit(solution)/shard_map/ppermute | solution.py:41
  407.2 27.0 %copy-start.6 = (f32[128,1024]{0,1:T(8,128)}, f32[128,1024]{0,1:T(8,128)S(1)}, u32[]{:S(2)}) copy-start(f32[128,1024]{0,1:T(8,128)S(1)} %collective-permute-done.3) | copy-start | bytes 1572868
  407.2 13.6 %collective-permute-start.4 = (f32[128,1024]{0,1:T(8,128)S(1)}, f32[128,1024]{0,1:T(8,128)S(1)}, u32[]{:S(2)}, u32[]{:S(2)}) collective-permute-start(f32[128,1024]{0,1:T(8,128)S(1)} %collective-permute-done.3), channel_id=1, source_target_pairs={{0,1},{1,2},{2,3},{3,4},{4,5},{5,6},{6,7},{7,8},{8,9},{9,10},{10,1... | collective-permute-start | bytes 1572872 | tf_op jit(solution)/shard_map/ppermute | solution.py:39
  407.2 0.9 copy-start.2
  408.0 12.8 %collective-permute-start.11 = (f32[128,1024]{0,1:T(8,128)S(1)}, f32[128,1024]{0,1:T(8,128)S(1)}, u32[]{:S(2)}, u32[]{:S(2)}) collective-permute-start(f32[128,1024]{0,1:T(8,128)S(1)} %collective-permute-done.10), channel_id=1, source_target_pairs={{1,0},{2,1},{3,2},{4,3},{5,4},{6,5},{7,6},{8,7},{9,8},{10,9},{11,1... | collective-permute-start | bytes 1572872 | tf_op jit(solution)/shard_map/ppermute | solution.py:41
  420.8 19.3 %copy-start.8 = (f32[128,1024]{0,1:T(8,128)}, f32[128,1024]{0,1:T(8,128)S(1)}, u32[]{:S(2)}) copy-start(f32[128,1024]{0,1:T(8,128)S(1)} %collective-permute-done.4) | copy-start | bytes 1572868
  420.8 12.7 %collective-permute-start.5 = (f32[128,1024]{0,1:T(8,128)S(1)}, f32[128,1024]{0,1:T(8,128)S(1)}, u32[]{:S(2)}, u32[]{:S(2)}) collective-permute-start(f32[128,1024]{0,1:T(8,128)S(1)} %collective-permute-done.4), channel_id=1, source_target_pairs={{0,1},{1,2},{2,3},{3,4},{4,5},{5,6},{6,7},{7,8},{8,9},{9,10},{10,1... | collective-permute-start | bytes 1572872 | tf_op jit(solution)/shard_map/ppermute | solution.py:39
  420.8 0.9 copy-start.4
  421.7 12.4 %collective-permute-start.12 = (f32[128,1024]{0,1:T(8,128)S(1)}, f32[128,1024]{0,1:T(8,128)}, u32[]{:S(2)}, u32[]{:S(2)}) collective-permute-start(f32[128,1024]{0,1:T(8,128)S(1)} %collective-permute-done.11), channel_id=1, source_target_pairs={{1,0},{2,1},{3,2},{4,3},{5,4},{6,5},{7,6},{8,7},{9,8},{10,9},{11,1... | collective-permute-start | bytes 1572872 | tf_op jit(solution)/shard_map/ppermute | solution.py:41
  433.5 12.8 %copy-start.9 = (f32[128,1024]{0,1:T(8,128)}, f32[128,1024]{0,1:T(8,128)S(1)}, u32[]{:S(2)}) copy-start(f32[128,1024]{0,1:T(8,128)S(1)} %collective-permute-done.5) | copy-start | bytes 1572868
  433.5 12.8 %collective-permute-start.6 = (f32[128,1024]{0,1:T(8,128)S(1)}, f32[128,1024]{0,1:T(8,128)}, u32[]{:S(2)}, u32[]{:S(2)}) collective-permute-start(f32[128,1024]{0,1:T(8,128)S(1)} %collective-permute-done.5), channel_id=1, source_target_pairs={{0,1},{1,2},{2,3},{3,4},{4,5},{5,6},{6,7},{7,8},{8,9},{9,10},{10,1... | collective-permute-start | bytes 1572872 | tf_op jit(solution)/shard_map/ppermute | solution.py:39
  434.2 13.5 %collective-permute-start.13 = (f32[128,1024]{0,1:T(8,128)}, f32[128,1024]{0,1:T(8,128)}, u32[]{:S(2)}, u32[]{:S(2)}) collective-permute-start(f32[128,1024]{0,1:T(8,128)} %collective-permute-done.12), channel_id=1, source_target_pairs={{1,0},{2,1},{3,2},{4,3},{5,4},{6,5},{7,6},{8,7},{9,8},{10,9},{11,1... | collective-permute-start | bytes 1572872 | tf_op jit(solution)/shard_map/ppermute | solution.py:41
  446.3 12.8 %collective-permute-start.7 = (f32[128,1024]{0,1:T(8,128)}, f32[128,1024]{0,1:T(8,128)}, u32[]{:S(2)}, u32[]{:S(2)}) collective-permute-start(f32[128,1024]{0,1:T(8,128)} %collective-permute-done.6), channel_id=1, source_target_pairs={{0,1},{1,2},{2,3},{3,4},{4,5},{5,6},{6,7},{7,8},{8,9},{9,10},{10,1... | collective-permute-start | bytes 1572872 | tf_op jit(solution)/shard_map/ppermute | solution.py:39
  446.3 20.3 %copy-start.7 = (f32[128,1024]{0,1:T(8,128)S(1)}, f32[128,1024]{0,1:T(8,128)}, u32[]{:S(2)}) copy-start(f32[128,1024]{0,1:T(8,128)} %copy-done.6) | copy-start | bytes 1572868
  447.6 30.2 %collective-permute-start.14 = (f32[128,1024]{0,1:T(8,128)}, f32[128,1024]{0,1:T(8,128)S(1)}, u32[]{:S(2)}, u32[]{:S(2)}) collective-permute-start(f32[128,1024]{0,1:T(8,128)} %collective-permute-done.13), channel_id=1, source_target_pairs={{1,0},{2,1},{3,2},{4,3},{5,4},{6,5},{7,6},{8,7},{9,8},{10,9},{11,1... | collective-permute-start | bytes 1572872 | tf_op jit(solution)/shard_map/ppermute | solution.py:41
  464.7 7.7 %copy-start.3 = (f32[128,1024]{0,1:T(8,128)S(1)}, f32[128,1024]{0,1:T(8,128)}, u32[]{:S(2)}) copy-start(f32[128,1024]{0,1:T(8,128)} %copy-done.2) | copy-start | bytes 1572868
  466.7 6.6 %copy-start.5 = (f32[128,1024]{0,1:T(8,128)S(1)}, f32[128,1024]{0,1:T(8,128)}, u32[]{:S(2)}) copy-start(f32[128,1024]{0,1:T(8,128)} %copy-done.4) | copy-start | bytes 1572868
  500.6 1.0 copy-start.10
Sparse Core Ops, SparseCore 0:
  500.8 69.7 all-reduce.2
